TPU v7x, 256 devices: a whole 4x4x8 slice. The times are simulated.
256 devices in a mesh: row: 16 (over y_hi, z), col: 16 (over x, y_lo, core).
Axes of the slice: x: 4, y: 4 (y_hi: 2, y_lo: 2; y = y_hi * 2 + y_lo), z: 8, core: 2. Of those that a mesh axis runs over, the one named last changes fastest.
Arguments:
- lesser: bfloat16 [16384, 16384], P('row', 'col'), may hold values from -6 to 6
- greater: bfloat16 [16384, 16384], P('row', 'col'), may hold values from -6 to 6
- screened_lesser: bfloat16 [16384, 16384], P('row', 'col'), may hold values from -6 to 6
- screened_greater: bfloat16 [16384, 16384], P('row', 'col'), may hold values from -6 to 6
Outputs:
- collision: float32 [16384, 4096], P('row', 'col')
All inputs are finite; a program needn't handle non-finite values.
Results may differ from a plain program's by a relative error of at most 0.0051.
Values may be sent and summed in bfloat16 or wider, within the bound.
A program may use at most 64 MiB of HBM per device.

v0:
```python
import jax
import jax.numpy as jnp
from jax import lax
from jax.sharding import PartitionSpec as P

WINDOW = 256


def carried_in(part, axis, combine, identity):
    place = lax.axis_index(axis)
    gathered = lax.all_gather(part, axis)
    state = jnp.zeros_like(part) + jnp.asarray(identity, part.dtype)

    def one(hop, state):
        return combine(state, lax.dynamic_index_in_dim(gathered, hop, 0, False))

    return lax.fori_loop(0, place, one, state)


def add_terms(first, second):
    return first + second


def local(lesser, greater, screened_lesser, screened_greater):
    row_count, tile_width = lesser.shape
    row_devices = lax.axis_size("row")
    col_devices = lax.axis_size("col")
    ratio = row_devices // col_devices
    my_row = lax.axis_index("row")
    my_col = lax.axis_index("col")
    scale = float(tile_width * col_devices) ** (-0.5)
    green_part = lesser.reshape(row_count, ratio, row_count)[:, :, :WINDOW]
    great_part = greater.reshape(row_count, ratio, row_count)[:, :, :WINDOW]
    diff_part = (green_part.astype(jnp.float32) - great_part.astype(jnp.float32)).astype(
        jnp.bfloat16
    )
    piece_rows = row_count // col_devices
    first_green = green_part.reshape(col_devices, piece_rows, ratio, WINDOW)
    first_diff = diff_part.reshape(col_devices, piece_rows, ratio, WINDOW)
    spread = (
        lax.all_to_all(first_green, "col", split_axis=0, concat_axis=0, tiled=True),
        lax.all_to_all(first_diff, "col", split_axis=0, concat_axis=0, tiled=True),
    )

    def to_rows(block):
        return jnp.transpose(block, (0, 2, 1, 3)).reshape(1, row_devices, piece_rows, WINDOW)

    crossed = (
        lax.all_to_all(to_rows(spread[0]), "row", split_axis=1, concat_axis=0, tiled=True),
        lax.all_to_all(to_rows(spread[1]), "row", split_axis=1, concat_axis=0, tiled=True),
    )

    def to_cols(block):
        return jnp.transpose(block, (1, 0, 2, 3))

    settled = (
        lax.all_to_all(to_cols(crossed[0]), "col", split_axis=1, concat_axis=1, tiled=True),
        lax.all_to_all(to_cols(crossed[1]), "col", split_axis=1, concat_axis=1, tiled=True),
    )
    green_win = settled[0].reshape(tile_width, WINDOW)
    diff_win = settled[1].reshape(tile_width, WINDOW)
    inner_times = my_col * tile_width + jnp.arange(tile_width, dtype=jnp.int32)
    window_times = my_row * row_count + jnp.arange(WINDOW, dtype=jnp.int32)
    diff_win = jnp.where(
        inner_times[:, None] <= window_times[None, :], diff_win, jnp.zeros((), jnp.bfloat16)
    )
    later_times = my_row * row_count + jnp.arange(row_count, dtype=jnp.int32)
    prod_less = lesser.astype(jnp.float32) * screened_lesser.astype(jnp.float32)
    prod_great = greater.astype(jnp.float32) * screened_greater.astype(jnp.float32)
    sigma_less = prod_less.astype(jnp.bfloat16)
    sigma_ret = jnp.where(
        inner_times[None, :] <= later_times[:, None], prod_great - prod_less, 0.0
    ).astype(jnp.bfloat16)
    partial_value = jnp.dot(sigma_ret, green_win, preferred_element_type=jnp.float32)
    partial_value = partial_value + jnp.dot(
        sigma_less, diff_win, preferred_element_type=jnp.float32
    )
    partial_value = scale * partial_value
    earlier = carried_in(partial_value, "col", add_terms, jnp.zeros_like(partial_value))
    collision = earlier + partial_value
    return collision


def solution(mesh):
    in_specs = (P("row", "col"), P("row", "col"), P("row", "col"), P("row", "col"))
    out_specs = P("row", "col")
    return jax.shard_map(local, mesh=mesh, in_specs=in_specs, out_specs=out_specs, check_vma=False)
```

profile of v0, /device:TPU:15, one launch (start us, length us, event | category | flops | bytes accessed | tf_op | source)
XLA Modules:
  0.0 238.2 jit_solution(3138558062530381869)
XLA Ops:
  6.5 0.0 copy-start.1
  6.5 2.3 subtract_convert_fusion
  8.8 6.0 %all-to-all-start.3 = ((bf16[16,64,1,256]{3,1,2,0:T(8,128)(2,1)}), bf16[16,64,1,256]{3,1,2,0:T(8,128)(2,1)S(1)}, u32[]{:S(2)}, u32[]{:S(2)}) async-start(bf16[16,64,1,256]{3,1,2,0:T(8,128)(2,1)} %bitcast.7), calls=%async_computation.3 | async-start | bytes 1048576 | tf_op jit(solution)/shard_map/all_to_all | solution.py:42
  14.8 0.0 copy-done.1
  14.8 0.1 slice.8
  14.9 7.0 %all-to-all-done.3 = bf16[16,64,1,256]{3,1,2,0:T(8,128)(2,1)S(1)} async-done(((bf16[16,64,1,256]{3,1,2,0:T(8,128)(2,1)}), bf16[16,64,1,256]{3,1,2,0:T(8,128)(2,1)S(1)}, u32[]{:S(2)}, u32[]{:S(2)}) %all-to-all-start.3) | async-done | bytes 524320 | tf_op jit(solution)/shard_map/all_to_all | solution.py:42
  21.9 13.4 %all_to_all.38 = bf16[16,64,1,256]{3,1,2,0:T(8,128)(2,1)S(1)} all-to-all(bf16[16,64,1,256]{3,1,2,0:T(8,128)(2,1)S(1)} %bitcast.22), channel_id=1, replica_groups=mesh['row'=16,'col'=16] {'col'}, dimensions={0} | all-to-all | bytes 1048576 | tf_op jit(solution)/shard_map/all_to_all | solution.py:41
  35.3 25.2 %all_to_all.39 = bf16[1,16,64,256]{3,2,0,1:T(8,128)(2,1)} all-to-all(bf16[1,16,64,256]{3,2,0,1:T(8,128)(2,1)S(1)} %bitcast.21), channel_id=1, replica_groups=mesh['row'=16,'col'=16] {'row'}, dimensions={1} | all-to-all | bytes 1048576 | tf_op jit(solution)/shard_map/all_to_all | solution.py:50
  60.5 20.2 %all_to_all.40 = bf16[1,16,64,256]{3,2,0,1:T(8,128)(2,1)} all-to-all(bf16[1,16,64,256]{3,2,0,1:T(8,128)(2,1)S(1)} %bitcast.23), channel_id=1, replica_groups=mesh['row'=16,'col'=16] {'row'}, dimensions={1} | all-to-all | bytes 1048576 | tf_op jit(solution)/shard_map/all_to_all | solution.py:49
  80.8 10.4 %all-to-all-start.2 = ((bf16[1,16,64,256]{3,2,0,1:T(8,128)(2,1)}), bf16[1,16,64,256]{3,2,0,1:T(8,128)(2,1)S(1)}, u32[]{:S(2)}, u32[]{:S(2)}) async-start(bf16[1,16,64,256]{3,2,0,1:T(8,128)(2,1)} %all_to_all.40), calls=%async_computation.2 | async-start | bytes 1048576 | tf_op jit(solution)/shard_map/all_to_all | solution.py:57
  91.2 7.1 %all-to-all-done.2 = bf16[1,16,64,256]{3,2,0,1:T(8,128)(2,1)S(1)} async-done(((bf16[1,16,64,256]{3,2,0,1:T(8,128)(2,1)}), bf16[1,16,64,256]{3,2,0,1:T(8,128)(2,1)S(1)}, u32[]{:S(2)}, u32[]{:S(2)}) %all-to-all-start.2) | async-done | bytes 524320 | tf_op jit(solution)/shard_map/all_to_all | solution.py:57
  98.3 7.3 %all-to-all-start.5 = ((bf16[1,16,64,256]{3,2,0,1:T(8,128)(2,1)}), bf16[1,16,64,256]{3,2,0,1:T(8,128)(2,1)S(1)}, u32[]{:S(2)}, u32[]{:S(2)}) async-start(bf16[1,16,64,256]{3,2,0,1:T(8,128)(2,1)} %all_to_all.39), calls=%async_computation.5 | async-start | bytes 1048576 | tf_op jit(solution)/shard_map/all_to_all | solution.py:58
  105.6 0.0 all-gather.3.cloned.1.call-start
  105.6 5.2 %fusion.3 = f32[1024,256]{1,0:T(8,128)} fusion(bf16[1024,256]{1,0:T(8,128)(2,1)S(1)} %bitcast.25, bf16[1024,1024]{1,0:T(8,128)(2,1)} %param.9, bf16[1024,1024]{1,0:T(8,128)(2,1)} %param.7, bf16[1024,1024]{1,0:T(8,128)(2,1)} %param.8, bf16[1024,1024]{1,0:T(8,128)(2,1)S(1)} %copy-done.1, s32[1024]{0:T(1024)S(1)} %get-tuple-element.38, ...), kind=kOutput, calls=%fused_computation.5 | convolution fusion | flops 547356672 | bytes 9969664 | tf_op jit(solution)/shard_map/dot_general | solution.py:74
  110.8 1.8 all-to-all-done.5
  112.7 3.7 %fusion.8 = f32[1024,256]{1,0:T(8,128)} fusion(f32[1024,256]{1,0:T(8,128)} %fusion.3, bf16[1024,1024]{1,0:T(8,128)(2,1)} %param.8, bf16[1024,1024]{1,0:T(8,128)(2,1)S(1)} %copy-done.1, bf16[1024,256]{1,0:T(8,128)(2,1)S(1)} %bitcast.20, s32[256]{0:T(256)S(1)} %iota_add_fusion.2, s32[1024]{0:T(1024)S(1)} %get-tuple-element.38), kind=kOutput, calls=%fused_computation.8 | convolution fusion | flops 542113792 | bytes 6820864 | tf_op jit(solution)/shard_map/dot_general | solution.py:75
  116.4 0.0 all-gather.3.cloned.1.call-update
  116.4 91.5 %all-gather.3.cloned.1.call-done = f32[16384,256]{1,0:T(8,128)} async-done(((f32[1024,256]{1,0:T(8,128)}), f32[16384,256]{1,0:T(8,128)}) %all-gather.3.cloned.1.call-update) | async-done | bytes 16777232 | tf_op jit(solution)/shard_map/all_gather | solution.py:11
  207.9 0.1 broadcast_in_dim.15
  208.0 0.0 copy-start
  208.0 22.2 %while.10 = (s32[]{:T(128)}, f32[1024,256]{1,0:T(8,128)S(1)}, s32[]{:T(128)}, f32[16,1024,256]{2,1,0:T(8,128)}, s32[]{:T(128)}, /*index=5*/s32[]{:T(128)}, s32[]{:T(128)}) while((s32[]{:T(128)}, f32[1024,256]{1,0:T(8,128)S(1)}, s32[]{:T(128)}, f32[16,1024,256]{2,1,0:T(8,128)}, s32[]{:T(128)}, /*index=5*/s32[]{:T(128)}, s32[]{:T(128)}) %tuple.24), condition=%wide.region_1.2_spmd, body=%wide.region_0.1_spmd.sunk | while | flops 262149 | bytes 3145851 | solution.py:17
  208.0 1.5 bitcast_add_fusion.2
  209.6 1.5 bitcast_add_fusion.2
  211.1 1.5 bitcast_add_fusion.2
  212.5 1.5 bitcast_add_fusion.2
  214.0 1.5 bitcast_add_fusion.2
  215.5 1.5 bitcast_add_fusion.2
  217.0 1.5 bitcast_add_fusion.2
  218.4 1.5 bitcast_add_fusion.2
  219.9 1.5 bitcast_add_fusion.2
  221.4 1.5 bitcast_add_fusion.2
  222.9 1.5 bitcast_add_fusion.2
  224.3 1.5 bitcast_add_fusion.2
  225.8 1.5 bitcast_add_fusion.2
  227.3 1.5 bitcast_add_fusion.2
  228.8 1.5 bitcast_add_fusion.2
  230.2 0.0 copy-done
  230.2 1.1 add.57
  (2 shorter events, 0.0 us)
Async XLA Ops:
  6.5 8.3 %copy-start.1 = (bf16[1024,1024]{1,0:T(8,128)(2,1)S(1)}, bf16[1024,1024]{1,0:T(8,128)(2,1)}, u32[]{:S(2)}) copy-start(bf16[1024,1024]{1,0:T(8,128)(2,1)} %param.6) | copy-start | bytes 6291460
  8.8 13.1 %all-to-all-start.3 = ((bf16[16,64,1,256]{3,1,2,0:T(8,128)(2,1)}), bf16[16,64,1,256]{3,1,2,0:T(8,128)(2,1)S(1)}, u32[]{:S(2)}, u32[]{:S(2)}) async-start(bf16[16,64,1,256]{3,1,2,0:T(8,128)(2,1)} %bitcast.7), calls=%async_computation.3 | async-start | bytes 1048576 | tf_op jit(solution)/shard_map/all_to_all | solution.py:42
  80.8 17.5 %all-to-all-start.2 = ((bf16[1,16,64,256]{3,2,0,1:T(8,128)(2,1)}), bf16[1,16,64,256]{3,2,0,1:T(8,128)(2,1)S(1)}, u32[]{:S(2)}, u32[]{:S(2)}) async-start(bf16[1,16,64,256]{3,2,0,1:T(8,128)(2,1)} %all_to_all.40), calls=%async_computation.2 | async-start | bytes 1048576 | tf_op jit(solution)/shard_map/all_to_all | solution.py:57
  98.3 14.3 %all-to-all-start.5 = ((bf16[1,16,64,256]{3,2,0,1:T(8,128)(2,1)}), bf16[1,16,64,256]{3,2,0,1:T(8,128)(2,1)S(1)}, u32[]{:S(2)}, u32[]{:S(2)}) async-start(bf16[1,16,64,256]{3,2,0,1:T(8,128)(2,1)} %all_to_all.39), calls=%async_computation.5 | async-start | bytes 1048576 | tf_op jit(solution)/shard_map/all_to_all | solution.py:58
  105.6 102.3 %all-gather.3.cloned.1.call-start = ((), (), s32[]{:S(2)}) async-start(), calls=%async_computation.6 | async-start | bytes 17825792 | tf_op jit(solution)/shard_map/all_gather | solution.py:11
  208.0 22.3 %copy-start = (f32[1024,256]{1,0:T(8,128)S(1)}, f32[1024,256]{1,0:T(8,128)}, u32[]{:S(2)}) copy-start(f32[1024,256]{1,0:T(8,128)} %fusion.8) | copy-start | bytes 3145732
Sparse Core Ops, SparseCore 0:
  116.5 91.3 all-gather.2
where the time goes:
time: 239 us; the launch traced here: 238 us
  waiting for transfers between devices  108 us (45%)
  blocking collectives  58.9 us (25%)
  other arithmetic  25.3 us (11%)
  starting transfers between devices  23.7 us (10%)
  between operations  13.5 us (6%)
  matrix products  8.88 us (4%)
    all_gather x1, waiting for transfers between devices, carried_in(): gathered = lax.all_gather(part, axis)  91.5 us
    all_to_all x1, blocking collectives, local(): lax.all_to_all(to_rows(spread[1]), 'row', split_axis=1, concat_axis=0, ti...  25.2 us
    add x15, other arithmetic, add_terms(): return first + second  21.9 us
    all_to_all x1, blocking collectives, local(): lax.all_to_all(to_rows(spread[0]), 'row', split_axis=1, concat_axis=0, ti...  20.2 us
    all_to_all x1, blocking collectives, local(): lax.all_to_all(first_green, 'col', split_axis=0, concat_axis=0, tiled=True)  13.4 us
    all_to_all x1, starting transfers between devices, local(): lax.all_to_all(to_cols(crossed[0]), 'col', split_axis=1, concat_axis=1, t...  10.4 us
    all_to_all x1, starting transfers between devices, local(): lax.all_to_all(to_cols(crossed[1]), 'col', split_axis=1, concat_axis=1, t...  7.26 us
    all_to_all x1, waiting for transfers between devices, local(): lax.all_to_all(to_cols(crossed[0]), 'col', split_axis=1, concat_axis=1, t...  7.09 us
  transfers between devices with their start and end apart: 4, of which 4 were waited for; matrix products, arithmetic and copies ran while one was open for 2% of the time, Pallas kernels for 0%

commit v1 on v0

v1 whole, which is shorter than its diff:
```python
import functools

import jax
import jax.numpy as jnp
from jax import lax
from jax.experimental import pallas as pl
from jax.experimental.pallas import tpu as pltpu
from jax.sharding import PartitionSpec as P

WINDOW = 256
TILE = 1024
N = 16
CHIPS = 8
SCALE = 2.0**-7
MESH = pl.DeviceIdType.MESH

PLAN = (
    ((0, 0), (0, 2), (0, 14), (1, 2)),
    ((0, 0), (0, 12), (1, 2), (1, 14)),
    ((0, 0), (0, 4), (0, 6), (0, 12)),
)
PIECES = len(PLAN[0])
PIECE = TILE // PIECES
HALF = TILE // 2
PART = HALF // CHIPS


def pick(cls, values):
    out = jnp.int32(values[2])
    out = jnp.where(cls == 1, jnp.int32(values[1]), out)
    return jnp.where(cls == 0, jnp.int32(values[0]), out)


def kernel(
    less_hbm, great_hbm, wless_hbm, wgreat_hbm, out_ref,
    less, great, wless, wgreat, ret_s, less_s, win, slots, acc,
    pal, qsend, qrecv, esend, erecv, ysend, yrecv,
    load_sem, s1_send, s1_recv, f_send, win_recv,
    pal_send, pal_recv, q_send, q_recv, e_send, e_recv, y_send, y_recv,
):
    row = lax.axis_index("row")
    col = lax.axis_index("col")
    is_source = row < col
    is_lower = row > col
    works = row >= col
    core = col % 2
    chip = col // 2

    def at(r, c):
        return (r, c)

    barrier = pltpu.get_barrier_semaphore()

    def greet(r, c):
        pl.semaphore_signal(barrier, inc=1, device_id=at(r, c), device_id_type=MESH)

    relays = []
    count = jnp.int32(CHIPS)
    for j in range(1, PIECES):
        for cls in range(3):
            flip, mask = PLAN[cls][j]
            k = row ^ (8 * flip)
            r = col ^ mask
            a, b = ((0, 0), (0, 1), (1, 1))[cls]
            valid = (k < r) & (k // 8 == a) & (r // 8 == b)
            relays.append((cls, j, valid, k, r))
            count = count + valid.astype(jnp.int32)

            @pl.when(valid)
            def _():
                greet(k, r)

    cls_to = col // 8 + row // 8
    cls_from = row // 8 + col // 8
    count = count + jnp.where(is_source, PIECES, 0).astype(jnp.int32)

    @pl.when(is_lower)
    def _():
        for j in range(PIECES):
            f = pick(cls_to, [PLAN[c][j][0] for c in range(3)])
            m = pick(cls_to, [PLAN[c][j][1] for c in range(3)])
            greet(col ^ (8 * f), row ^ m)

    greet(row, col ^ 1)
    for d in range(1, CHIPS):
        greet(row, ((chip + d) % CHIPS) * 2 + core)

    STEPS = 4
    SR = TILE // STEPS

    def loads(i):
        rows = pl.ds(i * SR, SR)
        return [
            pltpu.make_async_copy(h.at[rows], v.at[rows], load_sem.at[i, n])
            for n, (h, v) in enumerate(
                ((less_hbm, less), (great_hbm, great), (wless_hbm, wless), (wgreat_hbm, wgreat))
            )
        ]

    def own_windows():
        out = []
        for j in range(PIECES):
            rows = pl.ds(j * PIECE, PIECE)
            for n, h in enumerate((less_hbm, great_hbm)):
                out.append(
                    pltpu.make_async_copy(
                        h.at[rows, pl.ds(0, WINDOW)], win.at[j, n], win_recv.at[j]
                    )
                )
        return out

    @pl.when(works)
    def _():
        for i in range(STEPS):
            for cp in loads(i):
                cp.start()

        @pl.when(row == col)
        def _():
            for cp in own_windows():
                cp.start()

        B = 16
        for i in range(STEPS):
            for cp in loads(i):
                cp.wait()

            @pl.loop(0, SR // B)
            def _(s):
                base = i * SR + s * B
                rows = pl.ds(pl.multiple_of(base, B), B)
                low = less[rows, :].astype(jnp.float32) * wless[rows, :].astype(jnp.float32)
                high = great[rows, :].astype(jnp.float32) * wgreat[rows, :].astype(jnp.float32)
                less_s[rows, :] = low.astype(jnp.bfloat16)
                later = row * TILE + base + lax.broadcasted_iota(jnp.int32, (B, TILE), 0)
                inner = col * TILE + lax.broadcasted_iota(jnp.int32, (B, TILE), 1)
                ret_s[rows, :] = jnp.where(inner <= later, high - low, 0.0).astype(jnp.bfloat16)

    pl.semaphore_wait(barrier, count)

    def first_sends(j, part):
        f = pick(cls_from, [PLAN[c][j][0] for c in range(3)])
        m = pick(cls_from, [PLAN[c][j][1] for c in range(3)])
        h = (less_hbm, great_hbm)[part]
        src = h.at[pl.ds(j * PIECE, PIECE), pl.ds(0, WINDOW)]
        if j == 0:
            return pltpu.make_async_remote_copy(
                src, win.at[0, part], s1_send.at[j, part], win_recv.at[0],
                device_id=at(col, row), device_id_type=MESH,
            )
        slot = (j - 1) * 3 + cls_from
        return pltpu.make_async_remote_copy(
            src, slots.at[slot, part], s1_send.at[j, part], s1_recv.at[slot],
            device_id=at(row ^ (8 * f), col ^ m), device_id_type=MESH,
        )

    @pl.when(is_source)
    def _():
        for j in range(PIECES):
            for part in range(2):
                first_sends(j, part).start()

    def forward(i):
        cls, j, valid, k, r = relays[i]
        return pltpu.make_async_remote_copy(
            slots.at[i], win.at[j], f_send.at[i], win_recv.at[j],
            device_id=at(r, k), device_id_type=MESH,
        )

    for i, (cls, j, valid, k, r) in enumerate(relays):
        @pl.when(valid)
        def _():
            pltpu.make_async_copy(slots.at[i], slots.at[i], s1_recv.at[i]).wait()
            forward(i).start()

    MB = 256

    @pl.when(works)
    def _():
        for j in range(PIECES):
            pltpu.make_async_copy(win.at[j], win.at[j], win_recv.at[j]).wait()
            green = win[j, 0]
            diff = (green.astype(jnp.float32) - win[j, 1].astype(jnp.float32)).astype(jnp.bfloat16)
            inner = col * TILE + j * PIECE + lax.broadcasted_iota(jnp.int32, (PIECE, WINDOW), 0)
            times = row * TILE + lax.broadcasted_iota(jnp.int32, (PIECE, WINDOW), 1)
            diff = jnp.where(inner <= times, diff, jnp.zeros((), jnp.bfloat16))
            us = pl.ds(j * PIECE, PIECE)

            @pl.loop(0, TILE // MB)
            def _(s):
                rows = pl.ds(pl.multiple_of(s * MB, MB), MB)
                value = jnp.dot(ret_s[rows, us], green, preferred_element_type=jnp.float32)
                value = value + jnp.dot(less_s[rows, us], diff, preferred_element_type=jnp.float32)
                value = value * SCALE
                if j == 0:
                    acc[rows, :] = value
                else:
                    acc[rows, :] = acc[rows, :] + value

    @pl.when(is_source)
    def _():
        acc[...] = jnp.zeros_like(acc)

    mine = pl.ds(pl.multiple_of(core * HALF, HALF), HALF)
    other = pl.ds(pl.multiple_of((1 - core) * HALF, HALF), HALF)
    pal_id = at(row, col ^ 1)
    pal_copy = pltpu.make_async_remote_copy(
        acc.at[other], pal, pal_send, pal_recv, device_id=pal_id, device_id_type=MESH
    )
    pal_copy.start()
    pal_copy.wait_recv()
    both = acc[mine, :] + pal[...]
    qsend[...] = both.astype(jnp.bfloat16).reshape(CHIPS, PART, WINDOW)

    def q_copy(d):
        to = (chip + d) % CHIPS
        return pltpu.make_async_remote_copy(
            qsend.at[to], qrecv.at[chip], q_send.at[d], q_recv.at[chip],
            device_id=at(row, to * 2 + core), device_id_type=MESH,
        )

    for d in range(1, CHIPS):
        q_copy(d).start()
    qrecv[chip] = qsend[chip]
    for d in range(1, CHIPS):
        src = (chip + CHIPS - d) % CHIPS
        pltpu.make_async_copy(qrecv.at[src], qrecv.at[src], q_recv.at[src]).wait()
    run = jnp.zeros((PART, WINDOW), jnp.float32)
    for m in range(CHIPS):
        esend[m] = run.astype(jnp.bfloat16)
        run = run + qrecv[m].astype(jnp.float32)

    def e_copy(d):
        to = (chip + d) % CHIPS
        return pltpu.make_async_remote_copy(
            esend.at[to], erecv.at[chip], e_send.at[d], e_recv.at[chip],
            device_id=at(row, to * 2 + core), device_id_type=MESH,
        )

    for d in range(1, CHIPS):
        e_copy(d).start()
    erecv[chip] = esend[chip]
    for d in range(1, CHIPS):
        src = (chip + CHIPS - d) % CHIPS
        pltpu.make_async_copy(erecv.at[src], erecv.at[src], e_recv.at[src]).wait()
    earlier = erecv[...].astype(jnp.float32).reshape(HALF, WINDOW)
    own = acc[mine, :]
    first = core == 0
    ysend[...] = earlier + jnp.where(first, own, 0.0)
    y_copy = pltpu.make_async_remote_copy(
        ysend, yrecv, y_send, y_recv, device_id=pal_id, device_id_type=MESH
    )
    y_copy.start()
    out_ref[mine, :] = earlier + own + jnp.where(first, 0.0, pal[...])
    y_copy.wait_recv()
    out_ref[other, :] = yrecv[...] + acc[other, :]

    @pl.when(is_source)
    def _():
        for j in range(PIECES):
            for part in range(2):
                first_sends(j, part).wait_send()

    for i, (cls, j, valid, k, r) in enumerate(relays):
        @pl.when(valid)
        def _():
            forward(i).wait_send()

    pal_copy.wait_send()
    y_copy.wait_send()
    for d in range(1, CHIPS):
        q_copy(d).wait_send()
        e_copy(d).wait_send()


def local(lesser, greater, screened_lesser, screened_greater):
    bf16, f32 = jnp.bfloat16, jnp.float32
    n_slots = 3 * (PIECES - 1)
    dma = pltpu.SemaphoreType.DMA
    return pl.pallas_call(
        kernel,
        out_shape=jax.ShapeDtypeStruct((TILE, WINDOW), f32),
        in_specs=[pl.BlockSpec(memory_space=pl.ANY)] * 4,
        out_specs=pl.BlockSpec(memory_space=pltpu.VMEM),
        scratch_shapes=[pltpu.VMEM((TILE, TILE), bf16)] * 6
        + [
            pltpu.VMEM((PIECES, 2, PIECE, WINDOW), bf16),
            pltpu.VMEM((n_slots, 2, PIECE, WINDOW), bf16),
            pltpu.VMEM((TILE, WINDOW), f32),
            pltpu.VMEM((HALF, WINDOW), f32),
            pltpu.VMEM((CHIPS, PART, WINDOW), bf16),
            pltpu.VMEM((CHIPS, PART, WINDOW), bf16),
            pltpu.VMEM((CHIPS, PART, WINDOW), bf16),
            pltpu.VMEM((CHIPS, PART, WINDOW), bf16),
            pltpu.VMEM((HALF, WINDOW), f32),
            pltpu.VMEM((HALF, WINDOW), f32),
            dma((4, 4)),
            dma((PIECES, 2)),
            dma((n_slots,)),
            dma((n_slots,)),
            dma((PIECES,)),
            dma(()),
            dma(()),
            dma((CHIPS,)),
            dma((CHIPS,)),
            dma((CHIPS,)),
            dma((CHIPS,)),
            dma(()),
            dma(()),
        ],
        compiler_params=pltpu.CompilerParams(
            collective_id=0, has_side_effects=True, vmem_limit_bytes=48 << 20
        ),
        name="collision",
    )(lesser, greater, screened_lesser, screened_greater)


def solution(mesh):
    spec = P("row", "col")
    return jax.shard_map(
        local, mesh=mesh, in_specs=(spec,) * 4, out_specs=spec, check_vma=False
    )
```

time: 239 us -> 73.2 us (0.31)
  the two profiles are of different devices: /device:TPU:15 before, /device:TPU:157 now
where the time goes in v1:
time: 73.2 us; the launch traced here: 73.1 us
  Pallas kernels  68.9 us (94%)
  local copies, waits for them, and re-layouts  4.15 us (6%)
    pallas_call x1, Pallas kernels, local(): pl.pallas_call(kernel, out_shape=jax.ShapeDtypeStruct((TILE, WINDOW), f32...  68.9 us
    unnamed x5, local copies, waits for them, and re-layouts  4.15 us

profile of v1, /device:TPU:157, one launch (start us, length us, event | category | flops | bytes accessed | tf_op | source)
XLA Modules:
  0.0 73.1 jit_solution(7691658220101444701)
XLA Ops:
  0.0 0.0 copy-start
  0.0 1.6 %copy-done = bf16[1024,1024]{1,0:T(8,128)(2,1)S(1)} copy-done((bf16[1024,1024]{1,0:T(8,128)(2,1)S(1)}, bf16[1024,1024]{1,0:T(8,128)(2,1)}, u32[]{:S(2)}) %copy-start) | copy-done | bytes 2097176
  1.6 0.0 copy-start.1
  1.6 1.6 %copy-done.1 = bf16[1024,1024]{1,0:T(8,128)(2,1)S(1)} copy-done((bf16[1024,1024]{1,0:T(8,128)(2,1)S(1)}, bf16[1024,1024]{1,0:T(8,128)(2,1)}, u32[]{:S(2)}) %copy-start.1) | copy-done | bytes 2097176
  3.2 68.9 %collision.1 = f32[1024,256]{1,0:T(8,128)S(1)} custom-call(bf16[1024,1024]{1,0:T(8,128)(2,1)S(1)} %copy-done, bf16[1024,1024]{1,0:T(8,128)(2,1)S(1)} %copy-done.1, bf16[1024,1024]{1,0:T(8,128)(2,1)} %wless_hbm.1, bf16[1024,1024]{1,0:T(8,128)(2,1)} %wgreat_hbm.1), custom_call_target="tpu_custom_call" | custom-call | tf_op jit(solution)/shard_map/collision/pallas_call | solution.py:280
  72.1 1.0 %copy.6 = f32[1024,256]{1,0:T(8,128)} copy(f32[1024,256]{1,0:T(8,128)S(1)} %collision.1) | data formatting | bytes 2097152
Async XLA Ops:
  0.0 1.6 %copy-start = (bf16[1024,1024]{1,0:T(8,128)(2,1)S(1)}, bf16[1024,1024]{1,0:T(8,128)(2,1)}, u32[]{:S(2)}) copy-start(bf16[1024,1024]{1,0:T(8,128)(2,1)} %less_hbm.1) | copy-start | bytes 6291460
  1.6 1.6 %copy-start.1 = (bf16[1024,1024]{1,0:T(8,128)(2,1)S(1)}, bf16[1024,1024]{1,0:T(8,128)(2,1)}, u32[]{:S(2)}) copy-start(bf16[1024,1024]{1,0:T(8,128)(2,1)} %great_hbm.1) | copy-start | bytes 6291460

commit v2 on v1

--- a/solution.py
+++ b/solution.py
@@ -14,13 +14,12 @@
 SCALE = 2.0**-7
 MESH = pl.DeviceIdType.MESH
 
-PLAN = (
-    ((0, 0), (0, 2), (0, 14), (1, 2)),
-    ((0, 0), (0, 12), (1, 2), (1, 14)),
-    ((0, 0), (0, 4), (0, 6), (0, 12)),
-)
+PLAN = (((0, 0), (0, 2), (0, 4), (0, 6), (0, 14), (1, 0), (1, 2), (0, 3), (0, 5), (0, 7), (0, 15), (1, 3), (0, 2), (0, 4), (0, 6), (1, 2)), ((0, 0), (0, 2), (0, 4), (0, 6), (0, 8), (1, 0), (1, 2), (1, 4), (1, 6), (1, 14), (0, 9), (1, 1), (1, 3), (1, 7), (1, 15), (1, 14)), ((0, 0), (0, 2), (0, 4), (0, 6), (0, 8), (0, 12), (1, 0), (1, 2), (1, 4), (0, 5), (0, 9), (0, 13), (1, 1), (1, 3), (1, 5), (0, 12)))
 PIECES = len(PLAN[0])
 PIECE = TILE // PIECES
+GROUPS = 4
+GROUP = TILE // GROUPS
+PER = PIECES // GROUPS
 HALF = TILE // 2
 PART = HALF // CHIPS
 
@@ -35,7 +34,7 @@
     less_hbm, great_hbm, wless_hbm, wgreat_hbm, out_ref,
     less, great, wless, wgreat, ret_s, less_s, win, slots, acc,
     pal, qsend, qrecv, esend, erecv, ysend, yrecv,
-    load_sem, s1_send, s1_recv, f_send, win_recv,
+    near_sem, far_sem, load_sem, s1_send, s1_recv, f_send, win_recv,
     pal_send, pal_recv, q_send, q_recv, e_send, e_recv, y_send, y_recv,
 ):
     row = lax.axis_index("row")
@@ -55,7 +54,6 @@
         pl.semaphore_signal(barrier, inc=1, device_id=at(r, c), device_id_type=MESH)
 
     relays = []
-    count = jnp.int32(CHIPS)
     for j in range(1, PIECES):
         for cls in range(3):
             flip, mask = PLAN[cls][j]
@@ -64,26 +62,20 @@
             a, b = ((0, 0), (0, 1), (1, 1))[cls]
             valid = (k < r) & (k // 8 == a) & (r // 8 == b)
             relays.append((cls, j, valid, k, r))
-            count = count + valid.astype(jnp.int32)
-
-            @pl.when(valid)
-            def _():
-                greet(k, r)
-
-    cls_to = col // 8 + row // 8
     cls_from = row // 8 + col // 8
-    count = count + jnp.where(is_source, PIECES, 0).astype(jnp.int32)
-
-    @pl.when(is_lower)
-    def _():
-        for j in range(PIECES):
-            f = pick(cls_to, [PLAN[c][j][0] for c in range(3)])
-            m = pick(cls_to, [PLAN[c][j][1] for c in range(3)])
-            greet(col ^ (8 * f), row ^ m)
-
-    greet(row, col ^ 1)
-    for d in range(1, CHIPS):
-        greet(row, ((chip + d) % CHIPS) * 2 + core)
+
+    for d in range(1, N):
+        greet(row, (col + d) % N)
+    for d in range(N):
+        greet(row ^ 8, (col + d) % N)
+
+    def along(d):
+        return row // 8 * 8 + (row + d) % 8
+
+    near = (1, 2, 6, 7)
+    far = (3, 4, 5)
+    for d in near:
+        greet(along(d), col)
 
     STEPS = 4
     SR = TILE // STEPS
@@ -120,23 +112,7 @@
             for cp in own_windows():
                 cp.start()
 
-        B = 16
-        for i in range(STEPS):
-            for cp in loads(i):
-                cp.wait()
-
-            @pl.loop(0, SR // B)
-            def _(s):
-                base = i * SR + s * B
-                rows = pl.ds(pl.multiple_of(base, B), B)
-                low = less[rows, :].astype(jnp.float32) * wless[rows, :].astype(jnp.float32)
-                high = great[rows, :].astype(jnp.float32) * wgreat[rows, :].astype(jnp.float32)
-                less_s[rows, :] = low.astype(jnp.bfloat16)
-                later = row * TILE + base + lax.broadcasted_iota(jnp.int32, (B, TILE), 0)
-                inner = col * TILE + lax.broadcasted_iota(jnp.int32, (B, TILE), 1)
-                ret_s[rows, :] = jnp.where(inner <= later, high - low, 0.0).astype(jnp.bfloat16)
-
-    pl.semaphore_wait(barrier, count)
+    pl.semaphore_wait(barrier, 2 * N - 1 + len(near))
 
     def first_sends(j, part):
         f = pick(cls_from, [PLAN[c][j][0] for c in range(3)])
@@ -156,9 +132,44 @@
 
     @pl.when(is_source)
     def _():
-        for j in range(PIECES):
+        for j in range(1, PIECES):
             for part in range(2):
                 first_sends(j, part).start()
+
+    def tell(sem, steps):
+        for d in steps:
+            pl.semaphore_signal(
+                sem, inc=1, device_id=at(along(d), col), device_id_type=MESH
+            )
+
+    tell(near_sem, near)
+    pl.semaphore_wait(near_sem, len(near))
+    tell(far_sem, far)
+
+    @pl.when(works)
+    def _():
+        B = 16
+        for i in range(STEPS):
+            for cp in loads(i):
+                cp.wait()
+
+            @pl.loop(0, SR // B)
+            def _(s):
+                base = i * SR + s * B
+                rows = pl.ds(pl.multiple_of(base, B), B)
+                low = less[rows, :].astype(jnp.float32) * wless[rows, :].astype(jnp.float32)
+                high = great[rows, :].astype(jnp.float32) * wgreat[rows, :].astype(jnp.float32)
+                less_s[rows, :] = low.astype(jnp.bfloat16)
+                later = row * TILE + base + lax.broadcasted_iota(jnp.int32, (B, TILE), 0)
+                inner = col * TILE + lax.broadcasted_iota(jnp.int32, (B, TILE), 1)
+                ret_s[rows, :] = jnp.where(inner <= later, high - low, 0.0).astype(jnp.bfloat16)
+
+    pl.semaphore_wait(far_sem, len(far))
+
+    @pl.when(is_source)
+    def _():
+        for part in range(2):
+            first_sends(0, part).start()
 
     def forward(i):
         cls, j, valid, k, r = relays[i]
@@ -177,14 +188,17 @@
 
     @pl.when(works)
     def _():
-        for j in range(PIECES):
-            pltpu.make_async_copy(win.at[j], win.at[j], win_recv.at[j]).wait()
-            green = win[j, 0]
-            diff = (green.astype(jnp.float32) - win[j, 1].astype(jnp.float32)).astype(jnp.bfloat16)
-            inner = col * TILE + j * PIECE + lax.broadcasted_iota(jnp.int32, (PIECE, WINDOW), 0)
-            times = row * TILE + lax.broadcasted_iota(jnp.int32, (PIECE, WINDOW), 1)
+        for g in range(GROUPS):
+            for j in range(g * PER, (g + 1) * PER):
+                pltpu.make_async_copy(win.at[j], win.at[j], win_recv.at[j]).wait()
+            pieces = pl.ds(g * PER, PER)
+            green = win[pieces, 0].reshape(GROUP, WINDOW)
+            great_win = win[pieces, 1].reshape(GROUP, WINDOW).astype(jnp.float32)
+            diff = (green.astype(jnp.float32) - great_win).astype(jnp.bfloat16)
+            inner = col * TILE + g * GROUP + lax.broadcasted_iota(jnp.int32, (GROUP, WINDOW), 0)
+            times = row * TILE + lax.broadcasted_iota(jnp.int32, (GROUP, WINDOW), 1)
             diff = jnp.where(inner <= times, diff, jnp.zeros((), jnp.bfloat16))
-            us = pl.ds(j * PIECE, PIECE)
+            us = pl.ds(g * GROUP, GROUP)
 
             @pl.loop(0, TILE // MB)
             def _(s):
@@ -192,7 +206,7 @@
                 value = jnp.dot(ret_s[rows, us], green, preferred_element_type=jnp.float32)
                 value = value + jnp.dot(less_s[rows, us], diff, preferred_element_type=jnp.float32)
                 value = value * SCALE
-                if j == 0:
+                if g == 0:
                     acc[rows, :] = value
                 else:
                     acc[rows, :] = acc[rows, :] + value
@@ -294,6 +308,8 @@
             pltpu.VMEM((CHIPS, PART, WINDOW), bf16),
             pltpu.VMEM((HALF, WINDOW), f32),
             pltpu.VMEM((HALF, WINDOW), f32),
+            pltpu.SemaphoreType.REGULAR,
+            pltpu.SemaphoreType.REGULAR,
             dma((4, 4)),
             dma((PIECES, 2)),
             dma((n_slots,)),
@@ -309,7 +325,7 @@
             dma(()),
         ],
         compiler_params=pltpu.CompilerParams(
-            collective_id=0, has_side_effects=True, vmem_limit_bytes=48 << 20
+            collective_id=0, has_side_effects=True, vmem_limit_bytes=63 << 20
         ),
         name="collision",
     )(lesser, greater, screened_lesser, screened_greater)

time: 73.2 us -> 57.2 us (0.78)
  the two profiles are of different devices: /device:TPU:157 before, /device:TPU:17 now
where the time goes in v2:
time: 57.2 us; the launch traced here: 57.1 us
  Pallas kernels  54.8 us (96%)
  local copies, waits for them, and re-layouts  2.26 us (4%)
    pallas_call x1, Pallas kernels, local(): pl.pallas_call(kernel, out_shape=jax.ShapeDtypeStruct((TILE, WINDOW), f32...  54.8 us
    unnamed x1, local copies, waits for them, and re-layouts  2.26 us

profile of v2, /device:TPU:17, one launch (start us, length us, event | category | flops | bytes accessed | tf_op | source)
XLA Modules:
  0.0 57.1 jit_solution(14977900055184685041)
XLA Ops:
  0.0 54.8 %collision.1 = f32[1024,256]{1,0:T(8,128)} custom-call(bf16[1024,1024]{1,0:T(8,128)(2,1)} %less_hbm.1, bf16[1024,1024]{1,0:T(8,128)(2,1)} %great_hbm.1, bf16[1024,1024]{1,0:T(8,128)(2,1)} %wless_hbm.1, bf16[1024,1024]{1,0:T(8,128)(2,1)} %wgreat_hbm.1), custom_call_target="tpu_custom_call" | custom-call | tf_op jit(solution)/shard_map/collision/pallas_call | solution.py:294
  54.8 2.3 %copy.6 = f32[1024,256]{1,0:T(8,128)} copy(f32[1024,256]{1,0:T(8,128)} %collision.1) | data formatting | bytes 2097152

commit v3 on v2

--- a/solution.py
+++ b/solution.py
@@ -21,7 +21,9 @@
 GROUP = TILE // GROUPS
 PER = PIECES // GROUPS
 HALF = TILE // 2
-PART = HALF // CHIPS
+SUBS = 2
+SUB = HALF // SUBS
+PART = SUB // CHIPS
 
 
 def pick(cls, values):
@@ -33,7 +35,7 @@
 def kernel(
     less_hbm, great_hbm, wless_hbm, wgreat_hbm, out_ref,
     less, great, wless, wgreat, ret_s, less_s, win, slots, acc,
-    pal, qsend, qrecv, esend, erecv, ysend, yrecv,
+    psend, pal, qsend, qrecv, esend, erecv, ysend, yrecv,
     near_sem, far_sem, load_sem, s1_send, s1_recv, f_send, win_recv,
     pal_send, pal_recv, q_send, q_recv, e_send, e_recv, y_send, y_recv,
 ):
@@ -184,7 +186,35 @@
             pltpu.make_async_copy(slots.at[i], slots.at[i], s1_recv.at[i]).wait()
             forward(i).start()
 
-    MB = 256
+    pal_id = at(row, col ^ 1)
+    first = core == 0
+
+    def pal_copy(t):
+        return pltpu.make_async_remote_copy(
+            psend.at[t], pal.at[t], pal_send.at[t], pal_recv.at[t],
+            device_id=pal_id, device_id_type=MESH,
+        )
+
+    def q_copy(t, d):
+        to = (chip + d) % CHIPS
+        return pltpu.make_async_remote_copy(
+            qsend.at[t, to], qrecv.at[t, chip], q_send.at[t, d], q_recv.at[t, chip],
+            device_id=at(row, to * 2 + core), device_id_type=MESH,
+        )
+
+    def e_copy(t, to):
+        return pltpu.make_async_remote_copy(
+            esend.at[t, to], erecv.at[t, chip], e_send.at[t, to], e_recv.at[t, chip],
+            device_id=at(row, to * 2 + core), device_id_type=MESH,
+        )
+
+    def y_copy(t):
+        return pltpu.make_async_remote_copy(
+            ysend.at[t], yrecv.at[t], y_send.at[t], y_recv.at[t],
+            device_id=pal_id, device_id_type=MESH,
+        )
+
+    MB = 512
 
     @pl.when(works)
     def _():
@@ -202,72 +232,85 @@
 
             @pl.loop(0, TILE // MB)
             def _(s):
-                rows = pl.ds(pl.multiple_of(s * MB, MB), MB)
+                start = (s + core + 1) * MB % TILE
+                rows = pl.ds(pl.multiple_of(start, MB), MB)
                 value = jnp.dot(ret_s[rows, us], green, preferred_element_type=jnp.float32)
                 value = value + jnp.dot(less_s[rows, us], diff, preferred_element_type=jnp.float32)
                 value = value * SCALE
-                if g == 0:
-                    acc[rows, :] = value
-                else:
-                    acc[rows, :] = acc[rows, :] + value
+                if g > 0:
+                    value = acc[rows, :] + value
+                acc[rows, :] = value
+                if g == GROUPS - 1:
+                    @pl.when(s == 0)
+                    def _():
+                        psend[...] = value.astype(jnp.bfloat16).reshape(SUBS, SUB, WINDOW)
+                        for t in range(SUBS):
+                            pal_copy(t).start()
 
     @pl.when(is_source)
     def _():
         acc[...] = jnp.zeros_like(acc)
-
-    mine = pl.ds(pl.multiple_of(core * HALF, HALF), HALF)
-    other = pl.ds(pl.multiple_of((1 - core) * HALF, HALF), HALF)
-    pal_id = at(row, col ^ 1)
-    pal_copy = pltpu.make_async_remote_copy(
-        acc.at[other], pal, pal_send, pal_recv, device_id=pal_id, device_id_type=MESH
-    )
-    pal_copy.start()
-    pal_copy.wait_recv()
-    both = acc[mine, :] + pal[...]
-    qsend[...] = both.astype(jnp.bfloat16).reshape(CHIPS, PART, WINDOW)
-
-    def q_copy(d):
-        to = (chip + d) % CHIPS
-        return pltpu.make_async_remote_copy(
-            qsend.at[to], qrecv.at[chip], q_send.at[d], q_recv.at[chip],
-            device_id=at(row, to * 2 + core), device_id_type=MESH,
-        )
-
-    for d in range(1, CHIPS):
-        q_copy(d).start()
-    qrecv[chip] = qsend[chip]
-    for d in range(1, CHIPS):
-        src = (chip + CHIPS - d) % CHIPS
-        pltpu.make_async_copy(qrecv.at[src], qrecv.at[src], q_recv.at[src]).wait()
-    run = jnp.zeros((PART, WINDOW), jnp.float32)
-    for m in range(CHIPS):
-        esend[m] = run.astype(jnp.bfloat16)
-        run = run + qrecv[m].astype(jnp.float32)
-
-    def e_copy(d):
-        to = (chip + d) % CHIPS
-        return pltpu.make_async_remote_copy(
-            esend.at[to], erecv.at[chip], e_send.at[d], e_recv.at[chip],
-            device_id=at(row, to * 2 + core), device_id_type=MESH,
-        )
-
-    for d in range(1, CHIPS):
-        e_copy(d).start()
-    erecv[chip] = esend[chip]
-    for d in range(1, CHIPS):
-        src = (chip + CHIPS - d) % CHIPS
-        pltpu.make_async_copy(erecv.at[src], erecv.at[src], e_recv.at[src]).wait()
-    earlier = erecv[...].astype(jnp.float32).reshape(HALF, WINDOW)
-    own = acc[mine, :]
-    first = core == 0
-    ysend[...] = earlier + jnp.where(first, own, 0.0)
-    y_copy = pltpu.make_async_remote_copy(
-        ysend, yrecv, y_send, y_recv, device_id=pal_id, device_id_type=MESH
-    )
-    y_copy.start()
-    out_ref[mine, :] = earlier + own + jnp.where(first, 0.0, pal[...])
-    y_copy.wait_recv()
-    out_ref[other, :] = yrecv[...] + acc[other, :]
+        psend[...] = jnp.zeros_like(psend)
+        for t in range(SUBS):
+            pal_copy(t).start()
+
+    def sub_rows(half, t):
+        return pl.ds(pl.multiple_of(half * HALF + t * SUB, SUB), SUB)
+
+    last = CHIPS - 1
+
+    for t in range(SUBS):
+        pal_copy(t).wait_recv()
+        both = acc[sub_rows(core, t), :] + pal[t].astype(jnp.float32)
+        qsend[t] = both.astype(jnp.bfloat16).reshape(CHIPS, PART, WINDOW)
+
+        @pl.when(chip != last)
+        def _():
+            for d in range(1, CHIPS):
+                q_copy(t, d).start()
+
+        qrecv[t, chip] = qsend[t, chip]
+
+    for t in range(SUBS):
+        run = jnp.zeros((PART, WINDOW), jnp.float32)
+        for m in range(last):
+            @pl.when(chip != m)
+            def _():
+                pltpu.make_async_copy(qrecv.at[t, m], qrecv.at[t, m], q_recv.at[t, m]).wait()
+
+            run = run + qrecv[t, m].astype(jnp.float32)
+            esend[t, m + 1] = run.astype(jnp.bfloat16)
+
+            @pl.when(chip != m + 1)
+            def _():
+                e_copy(t, m + 1).start()
+
+        esend[t, 0] = jnp.zeros((PART, WINDOW), jnp.bfloat16)
+        erecv[t, chip] = esend[t, chip]
+
+    for t in range(SUBS):
+        @pl.when(chip == 0)
+        def _():
+            erecv[t] = jnp.zeros((CHIPS, PART, WINDOW), jnp.bfloat16)
+
+        @pl.when(chip != 0)
+        def _():
+            for m in range(CHIPS):
+                @pl.when(chip != m)
+                def _():
+                    pltpu.make_async_copy(erecv.at[t, m], erecv.at[t, m], e_recv.at[t, m]).wait()
+
+        earlier = erecv[t].astype(jnp.float32).reshape(SUB, WINDOW)
+        own = acc[sub_rows(core, t), :]
+        ysend[t] = (earlier + jnp.where(first, own, 0.0)).astype(jnp.bfloat16)
+        y_copy(t).start()
+        before = jnp.where(first, 0.0, pal[t].astype(jnp.float32))
+        out_ref[sub_rows(core, t), :] = earlier + before + own
+
+    for t in range(SUBS):
+        y_copy(t).wait_recv()
+        rows = sub_rows(1 - core, t)
+        out_ref[rows, :] = yrecv[t].astype(jnp.float32) + acc[rows, :]
 
     @pl.when(is_source)
     def _():
@@ -280,11 +323,19 @@
         def _():
             forward(i).wait_send()
 
-    pal_copy.wait_send()
-    y_copy.wait_send()
-    for d in range(1, CHIPS):
-        q_copy(d).wait_send()
-        e_copy(d).wait_send()
+    for t in range(SUBS):
+        pal_copy(t).wait_send()
+        y_copy(t).wait_send()
+
+        @pl.when(chip != last)
+        def _():
+            for d in range(1, CHIPS):
+                q_copy(t, d).wait_send()
+
+        for m in range(1, CHIPS):
+            @pl.when(chip != m)
+            def _():
+                e_copy(t, m).wait_send()
 
 
 def local(lesser, greater, screened_lesser, screened_greater):
@@ -301,13 +352,14 @@
             pltpu.VMEM((PIECES, 2, PIECE, WINDOW), bf16),
             pltpu.VMEM((n_slots, 2, PIECE, WINDOW), bf16),
             pltpu.VMEM((TILE, WINDOW), f32),
-            pltpu.VMEM((HALF, WINDOW), f32),
-            pltpu.VMEM((CHIPS, PART, WINDOW), bf16),
-            pltpu.VMEM((CHIPS, PART, WINDOW), bf16),
-            pltpu.VMEM((CHIPS, PART, WINDOW), bf16),
-            pltpu.VMEM((CHIPS, PART, WINDOW), bf16),
-            pltpu.VMEM((HALF, WINDOW), f32),
-            pltpu.VMEM((HALF, WINDOW), f32),
+            pltpu.VMEM((SUBS, SUB, WINDOW), bf16),
+            pltpu.VMEM((SUBS, SUB, WINDOW), bf16),
+            pltpu.VMEM((SUBS, CHIPS, PART, WINDOW), bf16),
+            pltpu.VMEM((SUBS, CHIPS, PART, WINDOW), bf16),
+            pltpu.VMEM((SUBS, CHIPS, PART, WINDOW), bf16),
+            pltpu.VMEM((SUBS, CHIPS, PART, WINDOW), bf16),
+            pltpu.VMEM((SUBS, SUB, WINDOW), bf16),
+            pltpu.VMEM((SUBS, SUB, WINDOW), bf16),
             pltpu.SemaphoreType.REGULAR,
             pltpu.SemaphoreType.REGULAR,
             dma((4, 4)),
@@ -315,14 +367,14 @@
             dma((n_slots,)),
             dma((n_slots,)),
             dma((PIECES,)),
-            dma(()),
-            dma(()),
-            dma((CHIPS,)),
-            dma((CHIPS,)),
-            dma((CHIPS,)),
-            dma((CHIPS,)),
-            dma(()),
-            dma(()),
+            dma((SUBS,)),
+            dma((SUBS,)),
+            dma((SUBS, CHIPS)),
+            dma((SUBS, CHIPS)),
+            dma((SUBS, CHIPS)),
+            dma((SUBS, CHIPS)),
+            dma((SUBS,)),
+            dma((SUBS,)),
         ],
         compiler_params=pltpu.CompilerParams(
             collective_id=0, has_side_effects=True, vmem_limit_bytes=63 << 20

time: 57.2 us -> 53.4 us (0.934)
  the two profiles are of different devices: /device:TPU:17 before, /device:TPU:21 now
where the time goes in v3:
time: 53.4 us; the launch traced here: 53.2 us
  Pallas kernels  51 us (96%)
  local copies, waits for them, and re-layouts  2.26 us (4%)
    pallas_call x1, Pallas kernels, local(): pl.pallas_call(kernel, out_shape=jax.ShapeDtypeStruct((TILE, WINDOW), f32...  51 us
    unnamed x1, local copies, waits for them, and re-layouts  2.26 us

profile of v3, /device:TPU:21, one launch (start us, length us, event | category | flops | bytes accessed | tf_op | source)
XLA Modules:
  0.0 53.2 jit_solution(5347032756717452770)
XLA Ops:
  0.0 51.0 %collision.1 = f32[1024,256]{1,0:T(8,128)} custom-call(bf16[1024,1024]{1,0:T(8,128)(2,1)} %less_hbm.1, bf16[1024,1024]{1,0:T(8,128)(2,1)} %great_hbm.1, bf16[1024,1024]{1,0:T(8,128)(2,1)} %wless_hbm.1, bf16[1024,1024]{1,0:T(8,128)(2,1)} %wgreat_hbm.1), custom_call_target="tpu_custom_call" | custom-call | tf_op jit(solution)/shard_map/collision/pallas_call | solution.py:345
  51.0 2.3 %copy.6 = f32[1024,256]{1,0:T(8,128)} copy(f32[1024,256]{1,0:T(8,128)} %collision.1) | data formatting | bytes 2097152

commit v4 on v3

--- a/solution.py
+++ b/solution.py
@@ -14,8 +14,22 @@
 SCALE = 2.0**-7
 MESH = pl.DeviceIdType.MESH
 
-PLAN = (((0, 0), (0, 2), (0, 4), (0, 6), (0, 14), (1, 0), (1, 2), (0, 3), (0, 5), (0, 7), (0, 15), (1, 3), (0, 2), (0, 4), (0, 6), (1, 2)), ((0, 0), (0, 2), (0, 4), (0, 6), (0, 8), (1, 0), (1, 2), (1, 4), (1, 6), (1, 14), (0, 9), (1, 1), (1, 3), (1, 7), (1, 15), (1, 14)), ((0, 0), (0, 2), (0, 4), (0, 6), (0, 8), (0, 12), (1, 0), (1, 2), (1, 4), (0, 5), (0, 9), (0, 13), (1, 1), (1, 3), (1, 5), (0, 12)))
+PLAN = (
+    (
+        (0, 0), (0, 2), (0, 4), (0, 6), (1, 2), (0, 14), (0, 3), (0, 5),
+        (0, 7), (1, 0), (1, 3), (0, 15), (0, 2), (0, 4), (0, 6), (1, 2),
+    ),
+    (
+        (0, 0), (1, 6), (1, 14), (0, 2), (0, 8), (1, 0), (0, 4), (1, 2),
+        (1, 4), (1, 7), (1, 15), (0, 3), (0, 9), (1, 1), (1, 6), (1, 14),
+    ),
+    (
+        (0, 0), (0, 12), (0, 2), (0, 4), (0, 8), (1, 0), (1, 4), (0, 13),
+        (1, 2), (1, 6), (0, 3), (0, 5), (0, 9), (1, 1), (1, 5), (0, 12),
+    ),
+)
 PIECES = len(PLAN[0])
+DIRECT = sum(way == (0, 0) for way in PLAN[0])
 PIECE = TILE // PIECES
 GROUPS = 4
 GROUP = TILE // GROUPS
@@ -56,7 +70,7 @@
         pl.semaphore_signal(barrier, inc=1, device_id=at(r, c), device_id_type=MESH)
 
     relays = []
-    for j in range(1, PIECES):
+    for j in range(DIRECT, PIECES):
         for cls in range(3):
             flip, mask = PLAN[cls][j]
             k = row ^ (8 * flip)
@@ -121,12 +135,12 @@
         m = pick(cls_from, [PLAN[c][j][1] for c in range(3)])
         h = (less_hbm, great_hbm)[part]
         src = h.at[pl.ds(j * PIECE, PIECE), pl.ds(0, WINDOW)]
-        if j == 0:
+        if j < DIRECT:
             return pltpu.make_async_remote_copy(
-                src, win.at[0, part], s1_send.at[j, part], win_recv.at[0],
+                src, win.at[j, part], s1_send.at[j, part], win_recv.at[j],
                 device_id=at(col, row), device_id_type=MESH,
             )
-        slot = (j - 1) * 3 + cls_from
+        slot = (j - DIRECT) * 3 + cls_from
         return pltpu.make_async_remote_copy(
             src, slots.at[slot, part], s1_send.at[j, part], s1_recv.at[slot],
             device_id=at(row ^ (8 * f), col ^ m), device_id_type=MESH,
@@ -134,7 +148,7 @@
 
     @pl.when(is_source)
     def _():
-        for j in range(1, PIECES):
+        for j in range(DIRECT, PIECES):
             for part in range(2):
                 first_sends(j, part).start()
 
@@ -170,8 +184,9 @@
 
     @pl.when(is_source)
     def _():
-        for part in range(2):
-            first_sends(0, part).start()
+        for j in range(DIRECT):
+            for part in range(2):
+                first_sends(j, part).start()
 
     def forward(i):
         cls, j, valid, k, r = relays[i]
@@ -340,7 +355,7 @@
 
 def local(lesser, greater, screened_lesser, screened_greater):
     bf16, f32 = jnp.bfloat16, jnp.float32
-    n_slots = 3 * (PIECES - 1)
+    n_slots = 3 * (PIECES - DIRECT)
     dma = pltpu.SemaphoreType.DMA
     return pl.pallas_call(
         kernel,

time: 53.4 us -> 51.2 us (0.959)
  Pallas kernels: 51 us -> 48.6 us
    pallas_call x1, Pallas kernels: 51 us -> 48.6 us  [local(): pl.pallas_call(kernel, out_shape=jax.ShapeDtypeStruct((TILE, WINDOW), f32...]
where the time goes in v4:
time: 51.2 us; the launch traced here: 50.9 us
  Pallas kernels  48.6 us (95%)
  local copies, waits for them, and re-layouts  2.26 us (4%)
    pallas_call x1, Pallas kernels, local(): pl.pallas_call(kernel, out_shape=jax.ShapeDtypeStruct((TILE, WINDOW), f32...  48.6 us
    unnamed x1, local copies, waits for them, and re-layouts  2.26 us

profile of v4, /device:TPU:21, one launch (start us, length us, event | category | flops | bytes accessed | tf_op | source)
XLA Modules:
  0.0 50.9 jit_solution(5296201005968277582)
XLA Ops:
  0.0 48.6 %collision.1 = f32[1024,256]{1,0:T(8,128)} custom-call(bf16[1024,1024]{1,0:T(8,128)(2,1)} %less_hbm.1, bf16[1024,1024]{1,0:T(8,128)(2,1)} %great_hbm.1, bf16[1024,1024]{1,0:T(8,128)(2,1)} %wless_hbm.1, bf16[1024,1024]{1,0:T(8,128)(2,1)} %wgreat_hbm.1), custom_call_target="tpu_custom_call" | custom-call | tf_op jit(solution)/shard_map/collision/pallas_call | solution.py:360
  48.6 2.3 %copy.6 = f32[1024,256]{1,0:T(8,128)} copy(f32[1024,256]{1,0:T(8,128)} %collision.1) | data formatting | bytes 2097152

commit v5 on v4

--- a/solution.py
+++ b/solution.py
@@ -80,10 +80,6 @@
             relays.append((cls, j, valid, k, r))
     cls_from = row // 8 + col // 8
 
-    for d in range(1, N):
-        greet(row, (col + d) % N)
-    for d in range(N):
-        greet(row ^ 8, (col + d) % N)
 
     def along(d):
         return row // 8 * 8 + (row + d) % 8
@@ -92,6 +88,10 @@
     far = (3, 4, 5)
     for d in near:
         greet(along(d), col)
+    for d in range(N):
+        greet(row ^ 8, (col + d + 8) % N)
+    for d in range(1, N):
+        greet(row, (col + d) % N)
 
     STEPS = 4
     SR = TILE // STEPS
@@ -392,7 +392,7 @@
             dma((SUBS,)),
         ],
         compiler_params=pltpu.CompilerParams(
-            collective_id=0, has_side_effects=True, vmem_limit_bytes=63 << 20
+            collective_id=0, has_side_effects=True, vmem_limit_bytes=65575000
         ),
         name="collision",
     )(lesser, greater, screened_lesser, screened_greater)

time: 51.2 us -> 51.1 us (level)
  no operation moved by 1% of the time
where the time goes in v5:
time: 51.1 us; the launch traced here: 50.8 us
  Pallas kernels  48.5 us (95%)
  local copies, waits for them, and re-layouts  2.26 us (4%)
    pallas_call x1, Pallas kernels, local(): pl.pallas_call(kernel, out_shape=jax.ShapeDtypeStruct((TILE, WINDOW), f32...  48.5 us
    unnamed x1, local copies, waits for them, and re-layouts  2.26 us

profile of v5, /device:TPU:21, one launch (start us, length us, event | category | flops | bytes accessed | tf_op | source)
XLA Modules:
  0.0 50.8 jit_solution(8161420200460201990)
XLA Ops:
  0.0 48.5 %collision.1 = f32[1024,256]{1,0:T(8,128)} custom-call(bf16[1024,1024]{1,0:T(8,128)(2,1)} %less_hbm.1, bf16[1024,1024]{1,0:T(8,128)(2,1)} %great_hbm.1, bf16[1024,1024]{1,0:T(8,128)(2,1)} %wless_hbm.1, bf16[1024,1024]{1,0:T(8,128)(2,1)} %wgreat_hbm.1), custom_call_target="tpu_custom_call" | custom-call | tf_op jit(solution)/shard_map/collision/pallas_call | solution.py:360
  48.6 2.3 %copy.6 = f32[1024,256]{1,0:T(8,128)} copy(f32[1024,256]{1,0:T(8,128)} %collision.1) | data formatting | bytes 2097152
